TPU v7x, 32 devices: a whole 2x2x4 slice. The times are simulated.
32 devices in a mesh: seq: 8 (over y, x, core), hid: 4 (over z).
Axes of the slice: x: 2, y: 2, z: 4, core: 2. Of those that a mesh axis runs over, the one named last changes fastest.
Arguments:
- projected: bfloat16 [2048, 3, 4096], P('seq', None, 'hid'), may hold values from -6 to 6
- short_taps: float32 [3, 3, 4096], P(None, None, 'hid'), may hold values from -3 to 3
- long_taps: bfloat16 [4096, 128], P('hid'), may hold values from -0.5 to 0.5
- skip_gain: float32 [4096], P('hid'), may hold values from 0.5 to 2
- out_weight: bfloat16 [4096, 4096], P('hid'), may hold values from -0.09375 to 0.09375
Outputs:
- mixer_out: bfloat16 [2048, 4096], P('seq', 'hid')
All inputs are finite; a program needn't handle non-finite values.
Results may differ from a plain program's by a relative error of at most 0.0095.
Values may be sent and summed in bfloat16 or wider, within the bound.
No kernel may reach another device: no remote copies, remote signals or barrier semaphores. Data moves between devices by JAX's collectives and lax.ppermute only.
A program may use at most 64 MiB of HBM per device.

v0:
```python
import jax
import jax.numpy as jnp
from jax import lax
from jax.sharding import PartitionSpec as P


def shifted(shard, axis, by):
    size = lax.axis_size(axis)
    pairs = [(i, i + by) for i in range(size) if 0 <= i + by < size]
    return lax.ppermute(shard, axis, pairs)


def short_filter(ext, taps):
    first = ext[2:].astype(jnp.float32)
    second = ext[1:-1].astype(jnp.float32)
    third = ext[:-2].astype(jnp.float32)
    return taps[0] * first + taps[1] * second + taps[2] * third


def causal_filter(extended, taps):
    channels = taps.shape[0]
    kernel = jnp.transpose(taps[:, ::-1])[:, None, :]
    result = lax.conv_general_dilated(
        extended[None],
        kernel,
        (1,),
        "VALID",
        dimension_numbers=("NWC", "WIO", "NWC"),
        feature_group_count=channels,
        preferred_element_type=jnp.float32,
    )
    return result[0]


def shards(projected, short_taps, long_taps, skip_gain, out_weight):
    tokens = projected.shape[0]
    length = long_taps.shape[1]
    tail = shifted(projected[tokens - length - 1 :], "seq", 1)
    ext = jnp.concatenate([tail, projected], axis=0)
    feat_all = short_filter(ext, short_taps)
    gated_all = (feat_all[:, 1] * feat_all[:, 2]).astype(jnp.bfloat16)
    halo_gated = gated_all[: length - 1]
    gated = gated_all[length - 1 :]
    query = feat_all[length - 1 :, 0]
    extended = jnp.concatenate([halo_gated, gated], axis=0)
    filtered = causal_filter(extended, long_taps) + skip_gain * gated.astype(jnp.float32)
    mixed = (query * filtered).astype(jnp.bfloat16)
    owned = lax.psum_scatter(
        lax.dot_general(
            out_weight, mixed, (((0,), (1,)), ((), ())), preferred_element_type=jnp.float32
        ).astype(jnp.bfloat16),
        "hid",
        scatter_dimension=0,
        tiled=True,
    ).astype(jnp.float32)
    return jnp.transpose(owned).astype(jnp.bfloat16)


def solution(mesh):
    placed = (P("seq", None, "hid"), P(None, None, "hid"), P("hid", None), P("hid"), P("hid", None))
    return jax.shard_map(
        shards, mesh=mesh, in_specs=placed, out_specs=P("seq", "hid"), check_vma=False
    )
```

profile of v0, /device:TPU:0, one launch (start us, length us, event | category | flops | bytes accessed | tf_op | source)
XLA Modules:
  0.0 97.4 jit_solution(16695058393760933893)
XLA Ops:
  6.5 0.0 reduce-scatter.2.cloned.1.call-start
  6.5 1.4 %slice.37 = bf16[129,3,1024]{2,0,1:T(8,128)(2,1)S(1)} slice(bf16[256,3,1024]{2,0,1:T(8,128)(2,1)} %param.5), slice={[127:256], [0:3], [0:1024]} | slice | bytes 1585152 | tf_op jit(solution)/shard_map/slice | solution.py:38
  7.9 2.4 %collective-permute-start = (bf16[129,3,1024]{2,0,1:T(8,128)(2,1)S(1)}, bf16[129,3,1024]{2,0,1:T(8,128)(2,1)S(1)}, u32[]{:S(2)}, u32[]{:S(2)}) collective-permute-start(bf16[129,3,1024]{2,0,1:T(8,128)(2,1)S(1)} %slice.37), channel_id=1, source_target_pairs={{0,4},{4,8},{8,12},{12,16},{16,20},{20,24},{24,28},{1,5},{5,9},{9,... | collective-permute-start | bytes 2377736 | tf_op jit(solution)/shard_map/ppermute | solution.py:10
  10.4 3.5 %rev.3 = bf16[1024,128]{1,0:T(8,128)(2,1)S(1)} reverse(bf16[1024,128]{1,0:T(8,128)(2,1)} %param.7), dimensions={1} | reverse | bytes 524288 | tf_op jit(solution)/shard_map/rev | solution.py:22
  13.9 0.5 copy.7
  14.4 0.8 slice_bitcast_fusion.5
  15.1 0.0 collective-permute-done
  15.1 3.8 %multiply_add_fusion = f32[383,3,1024]{2,0,1:T(8,128)S(1)} fusion(bf16[256,3,1024]{2,0,1:T(8,128)(2,1)} %param.5, bf16[129,3,1024]{2,0,1:T(8,128)(2,1)S(1)} %collective-permute-done, f32[3,1024]{1,0:T(4,128)S(1)} %get-tuple-element.6, f32[3,1024]{1,0:T(4,128)S(1)} %get-tuple-element.7, f32[3,1024]{1,0:T(4,128)S(1)} %get-tuple-element.5), kind=kLoop, calls=%fused_computation.2 | loop fusion | flops 20001792 | bytes 7108608 | tf_op jit(solution)/shard_map/add | solution.py:17
  19.0 0.2 fusion.12
  19.2 0.0 slice-start
  19.2 0.2 fusion.3
  19.4 0.0 slice-start.1
  19.5 0.0 copy-start
  19.5 14.1 %fusion.4 = f32[1,256,1024]{2,0,1:T(1,128)S(1)} fusion(bf16[128,1,1024]{2,1,0:T(2,128)(2,1)S(1)} %copy.7, bf16[1,383,1024]{2,1,0:T(8,128)(2,1)S(1)} %fusion.12), kind=kOutput, calls=%fused_computation.12 | convolution fusion | flops 67108864 | bytes 2095104 | tf_op jit(solution)/shard_map/conv_general_dilated | solution.py:23
  33.6 0.0 slice-done
  33.6 0.0 slice-done.1
  33.6 0.0 copy-done
  33.6 3.9 %fusion = bf16[4096,256]{0,1:T(8,128)(2,1)} fusion(bf16[1024,4096]{1,0:T(8,128)(2,1)S(1)} %bitcast.36, f32[383,3,1024]{2,0,1:T(8,128)S(1)} %multiply_add_fusion, f32[1,256,1024]{2,0,1:T(1,128)S(1)} %fusion.4, bf16[383,1,1024]{2,0,1:T(8,128)(2,1)S(1)} %fusion.3, f32[1024]{0:T(1024)S(1)} %copy-done), kind=kOutput, calls=%fused_computation.1 | convolution fusion | flops 2149842944 | bytes 13111296 | tf_op jit(solution)/shard_map/dot_general | solution.py:49
  37.5 0.0 reduce-scatter.2.cloned.1.call-update
  37.5 53.1 %reduce-scatter.2.cloned.1.call-done = bf16[1024,256]{0,1:T(8,128)(2,1)} async-done(((bf16[4096,256]{0,1:T(8,128)(2,1)}), bf16[1024,256]{0,1:T(8,128)(2,1)}) %reduce-scatter.2.cloned.1.call-update) | async-done | bytes 524304 | tf_op jit(solution)/shard_map/reduce_scatter | solution.py:48
  (1 shorter events, 0.0 us)
Async XLA Ops:
  6.5 84.0 %reduce-scatter.2.cloned.1.call-start = ((), (), s32[]{:S(2)}) async-start(), calls=%async_computation.1 | async-start | bytes 2621440 | tf_op jit(solution)/shard_map/reduce_scatter | solution.py:48
  7.9 7.2 %collective-permute-start = (bf16[129,3,1024]{2,0,1:T(8,128)(2,1)S(1)}, bf16[129,3,1024]{2,0,1:T(8,128)(2,1)S(1)}, u32[]{:S(2)}, u32[]{:S(2)}) collective-permute-start(bf16[129,3,1024]{2,0,1:T(8,128)(2,1)S(1)} %slice.37), channel_id=1, source_target_pairs={{0,4},{4,8},{8,12},{12,16},{16,20},{20,24},{24,28},{1,5},{5,9},{9,... | collective-permute-start | bytes 2377736 | tf_op jit(solution)/shard_map/ppermute | solution.py:10
  19.2 14.3 %slice-start = ((s8[8388608]{0:T(1024)(128)(4,1)}), s8[4194304]{0:T(1024)(128)(4,1)S(1)}, s32[]{:S(2)}) async-start(s8[8388608]{0:T(1024)(128)(4,1)} %bitcast.35), calls=%async_computation.2 | async-start | bytes 8388608
  19.4 14.1 %slice-start.1 = ((s8[8388608]{0:T(1024)(128)(4,1)}), s8[4194304]{0:T(1024)(128)(4,1)S(1)}, s32[]{:S(2)}) async-start(s8[8388608]{0:T(1024)(128)(4,1)} %bitcast.35), calls=%async_computation.3 | async-start | bytes 8388608
  19.5 14.1 %copy-start = (f32[1024]{0:T(1024)S(1)}, f32[1024]{0:T(1024)}, u32[]{:S(2)}) copy-start(f32[1024]{0:T(1024)} %param.8) | copy-start | bytes 12292
Sparse Core Ops, SparseCore 0:
  37.6 52.9 reduce-scatter.1
where the time goes:
time: 97.9 us; the launch traced here: 97.4 us
  waiting for transfers between devices  53.1 us (54%)
  matrix products  17.9 us (18%)
  between operations  13.5 us (14%)
  local copies, waits for them, and re-layouts  6.13 us (6%)
  other arithmetic  4.27 us (4%)
  starting transfers between devices  2.45 us (3%)
    reduce_scatter x1, waiting for transfers between devices, shards(): lax.psum_scatter(lax.dot_general(out_weight, mixed, (((0,), (1,)), ((), (...  53.1 us
    conv_general_dilated x1, matrix products, causal_filter(): lax.conv_general_dilated(extended[None], kernel, (1,), 'VALID', dimension...  14.1 us
    dot_general x1, matrix products, shards(): lax.dot_general(out_weight, mixed, (((0,), (1,)), ((), ())), preferred_el...  3.87 us
    add x1, other arithmetic, short_filter(): return taps[0] * first + taps[1] * second + taps[2] * third  3.84 us
    rev x1, local copies, waits for them, and re-layouts, causal_filter(): kernel = jnp.transpose(taps[:, ::-1])[:, None, :]  3.49 us
    ppermute x1, starting transfers between devices, shifted(): return lax.ppermute(shard, axis, pairs)  2.45 us
  transfers between devices with their start and end apart: 2, of which 1 were waited for; matrix products, arithmetic and copies ran while one was open for 5% of the time, Pallas kernels for 0%

commit v1 on v0

v1 whole, which is shorter than its diff:
```python
import functools

import jax
import jax.numpy as jnp
import numpy as np
from jax import lax
from jax.experimental import pallas as pl
from jax.experimental.pallas import tpu as pltpu
from jax.sharding import PartitionSpec as P

F32 = jnp.float32
BF16 = jnp.bfloat16
PAD = 16
STRIP = 256
ANY = pl.BlockSpec(memory_space=pl.ANY)


def split(values):
    high = values.astype(BF16)
    return high, (values - high.astype(F32)).astype(BF16)


def transforms(length):
    size = 2 * length
    angle = np.pi * (2 * np.arange(length)[:, None] + 1) * np.arange(size)[None] / size
    forward = np.concatenate([np.cos(angle), -np.sin(angle)]).astype(np.float32)
    inverse = np.concatenate([np.cos(angle), -np.sin(angle)]).T[length:] / length

    def halves(matrix):
        high = matrix.astype(BF16)
        return high, (matrix - high.astype(np.float64)).astype(BF16)

    return halves(forward.astype(np.float64)) + halves(inverse)


def matmul(a, b):
    return jnp.dot(a, b, preferred_element_type=F32)


def short_filter(ext, taps, rows):
    total = ext.shape[0]
    one = pltpu.roll(ext, 1, 0)
    two = pltpu.roll(ext, 2, 0)
    out = taps[0:1] * ext + taps[1:2] * one + taps[2:3] * two
    return out[total - rows :]


def spectrum_product(x, h):
    half = x.shape[0] // 2
    xr, xi, hr, hi = x[:half], x[half:], h[:half], h[half:]
    return jnp.concatenate([xr * hr - xi * hi, xr * hi + xi * hr])


def filter_window(window, h, fwd_hi, fwd_lo, inv_hi, inv_lo):
    x = matmul(fwd_hi, window) + matmul(fwd_lo, window)
    high, low = split(spectrum_product(x, h))
    return matmul(inv_hi, high) + matmul(inv_lo, high) + matmul(inv_hi, low)


def load_all(pairs, sems):
    copies = [pltpu.make_async_copy(src, dst, sems.at[i]) for i, (src, dst) in enumerate(pairs)]
    for copy in copies:
        copy.start()
    return copies


def column_block(weight, which, width):
    return weight.at[:, pl.ds(pl.multiple_of(which * width, width), width)]


def first_kernel(
    rows, width, proj, short, long_taps, skip, fh, fl, ih, il, weight,
    payload, mixed_out, gated_out, halo_out, h_out,
    k_buf, v_buf, q_buf, short_buf, long_buf, skip_buf, fh_buf, fl_buf, ih_buf, il_buf, w_buf, g_buf, m_buf, sems,
):
    me = lax.axis_index("hid")
    tokens, channels = k_buf.shape
    length = long_buf.shape[1]
    start = tokens - rows - PAD
    copies = load_all(
        [
            (short, short_buf), (proj.at[1], k_buf), (proj.at[2], v_buf), (fh, fh_buf), (fl, fl_buf),
            (long_taps, long_buf), (skip, skip_buf), (proj.at[0, start:], q_buf), (ih, ih_buf), (il, il_buf),
            (column_block(weight, me ^ 3, width), w_buf.at[0]), (column_block(weight, me ^ 1, width), w_buf.at[1]),
        ],
        sems,
    )
    for copy in copies[:10]:
        copy.wait()
    row = lax.broadcasted_iota(jnp.int32, (tokens, STRIP), 0)
    inv_hi = ih_buf[length - rows :]
    inv_lo = il_buf[length - rows :]
    for at in range(0, channels, STRIP):
        part = slice(at, at + STRIP)
        key = short_filter(k_buf[:, part].astype(F32), short_buf[:, 1, part], tokens)
        value = short_filter(v_buf[:, part].astype(F32), short_buf[:, 2, part], tokens)
        gated = jnp.where(row < 2, 0.0, key * value).astype(BF16)
        g_buf[:, part] = gated
        taps = long_buf[part]
        contract = (((1,), (1,)), ((), ()))
        h = lax.dot_general(fh_buf[:, :length], taps, contract, preferred_element_type=F32)
        h += lax.dot_general(fl_buf[:, :length], taps, contract, preferred_element_type=F32)
        h = jnp.concatenate([h[:length] + skip_buf[:, part], h[length:]])
        h_out[:, part] = h
        filtered = filter_window(gated, h, fh_buf[...], fl_buf[...], inv_hi, inv_lo)
        query = short_filter(q_buf[:, part].astype(F32), short_buf[:, 0, part], rows)
        m_buf[:, part] = (query * filtered).astype(BF16)
    gated_out[...] = g_buf[...]
    mixed_out[...] = m_buf[...]
    halo_out[:length] = g_buf[tokens - length :]
    halo_out[length : length + PAD] = q_buf[rows:]
    halo_out[length + PAD : length + 2 * PAD] = k_buf[tokens - PAD :]
    halo_out[length + 2 * PAD :] = v_buf[tokens - PAD :]
    for which in range(2):
        copies[10 + which].wait()
        payload[which] = matmul(m_buf[...], w_buf[which]).astype(BF16)


def later_kernel(
    begin, rows, back, width, proj, short, gated, halo, h, fh, fl, ih, il, weight,
    payload, mixed_out,
    head_buf, q_buf, short_buf, gated_buf, halo_buf, h_buf, fh_buf, fl_buf, ih_buf, il_buf, w_buf, m_buf, sems,
):
    me = lax.axis_index("hid")
    length, channels = halo_buf.shape[0] - 3 * PAD, halo_buf.shape[1]
    ahead = 2 * length - back
    low = begin - PAD if begin else 0
    copies = load_all(
        [
            (halo, halo_buf), (short, short_buf), (gated.at[:ahead], gated_buf), (proj.at[1:, :PAD], head_buf),
            (proj.at[0, low : begin + rows], q_buf), (h, h_buf), (fh, fh_buf), (fl, fl_buf), (ih, ih_buf), (il, il_buf),
            (column_block(weight, me ^ 3, width), w_buf.at[0]), (column_block(weight, me ^ 1, width), w_buf.at[1]),
        ],
        sems,
    )
    for copy in copies[:10]:
        copy.wait()
    first = begin + back - length
    inv_hi = ih_buf[first : first + rows]
    inv_lo = il_buf[first : first + rows]
    for at in range(0, channels, STRIP):
        part = slice(at, at + STRIP)

        def head(which, own):
            before = halo_buf[length + which * PAD : length + (which + 1) * PAD, part].astype(F32)
            return jnp.concatenate([before, own.astype(F32)])

        key = short_filter(head(1, head_buf[0, :, part]), short_buf[:, 1, part], PAD)
        value = short_filter(head(2, head_buf[1, :, part]), short_buf[:, 2, part], PAD)
        fixed = (key * value).astype(BF16)
        window = jnp.concatenate([halo_buf[length - back : length, part], fixed, gated_buf[PAD:, part]])
        filtered = filter_window(window, h_buf[:, part], fh_buf[...], fl_buf[...], inv_hi, inv_lo)
        ext = q_buf[:, part].astype(F32) if begin else head(0, q_buf[:, part])
        query = short_filter(ext, short_buf[:, 0, part], rows)
        m_buf[:, part] = (query * filtered).astype(BF16)
    mixed_out[...] = m_buf[...]
    for which in range(2):
        copies[10 + which].wait()
        payload[which] = matmul(m_buf[...], w_buf[which]).astype(BF16)


def keep_kernel(width, mixed, weight, out, w_buf, sems):
    me = lax.axis_index("hid")
    copies = load_all(
        [(column_block(weight, me ^ 2, width), w_buf.at[0]), (column_block(weight, me, width), w_buf.at[1])], sems
    )
    for which in range(2):
        copies[which].wait()
        out[which] = matmul(mixed[...], w_buf[which]).astype(BF16)


def shape(dims, dtype=BF16):
    return jax.ShapeDtypeStruct(dims, dtype)


def swapped(array, axis, mask):
    return lax.ppermute(array, axis, [(i, i ^ mask) for i in range(lax.axis_size(axis))])


def shards(projected, short_taps, long_taps, skip_gain, out_weight):
    tokens, _, channels = projected.shape
    length = long_taps.shape[1]
    width = out_weight.shape[1] // lax.axis_size("hid")
    proj = jnp.transpose(projected, (1, 0, 2))
    consts = [jnp.asarray(m) for m in transforms(length)]
    size = 2 * length
    const_bufs = [pltpu.VMEM(m.shape, BF16) for m in consts]
    w_bufs = pltpu.VMEM((2, channels, width), BF16)
    short_bufs = pltpu.VMEM(short_taps.shape, F32)
    halo_rows = length + 3 * PAD
    rows1 = tokens - length - PAD
    rows3 = length // 2
    rows2 = tokens - rows1 - rows3
    params = pltpu.CompilerParams(vmem_limit_bytes=56 << 20)

    pay1, mixed1, gated, halo, h = pl.pallas_call(
        functools.partial(first_kernel, rows1, width),
        name="first",
        out_shape=(
            shape((2, rows1, width)), shape((rows1, channels)), shape((tokens, channels)),
            shape((halo_rows, channels)), shape((size, channels), F32),
        ),
        in_specs=[ANY] * 9,
        scratch_shapes=[
            pltpu.VMEM((tokens, channels), BF16), pltpu.VMEM((tokens, channels), BF16),
            pltpu.VMEM((rows1 + PAD, channels), BF16), short_bufs, pltpu.VMEM((channels, length), BF16),
            pltpu.VMEM((1, channels), F32), *const_bufs, w_bufs,
            pltpu.VMEM((tokens, channels), BF16), pltpu.VMEM((rows1, channels), BF16), pltpu.SemaphoreType.DMA((12,)),
        ],
        compiler_params=params,
    )(proj, short_taps, long_taps, skip_gain[None], *consts, out_weight)

    got1 = swapped(pay1, "hid", 1)
    span = lax.axis_size("seq")
    before = lax.ppermute(halo, "seq", [(i, i + 1) for i in range(span - 1)])

    def later(begin, rows, back):
        q_rows = rows + PAD if begin else rows
        return pl.pallas_call(
            functools.partial(later_kernel, begin, rows, back, width),
            name=f"later{begin}",
            out_shape=(shape((2, rows, width)), shape((rows, channels))),
            in_specs=[ANY] * 10,
            scratch_shapes=[
                pltpu.VMEM((2, PAD, channels), BF16), pltpu.VMEM((q_rows, channels), BF16), short_bufs,
                pltpu.VMEM((size - back, channels), BF16), pltpu.VMEM((halo_rows, channels), BF16),
                pltpu.VMEM((size, channels), F32), *const_bufs, w_bufs,
                pltpu.VMEM((rows, channels), BF16), pltpu.SemaphoreType.DMA((12,)),
            ],
            compiler_params=params,
        )(proj, short_taps, gated, before, h, *consts, out_weight)

    def keep(mixed):
        return pl.pallas_call(
            functools.partial(keep_kernel, width),
            name="keep",
            out_shape=shape((2, mixed.shape[0], width)),
            in_specs=[pl.BlockSpec(memory_space=pltpu.VMEM), ANY],
            scratch_shapes=[w_bufs, pltpu.SemaphoreType.DMA((2,))],
            compiler_params=params,
        )(mixed, out_weight)

    pay2, mixed2 = later(rows3, rows2, length - PAD)
    got2 = swapped(pay2, "hid", 1)
    pay3, mixed3 = later(0, rows3, length)
    got3 = swapped(pay3, "hid", 1)

    def total(a, b):
        return (a.astype(F32) + b.astype(F32)).astype(BF16)

    pieces = []
    for got, mixed in ((got1, mixed1), (got2, mixed2), (got3, mixed3)):
        mine = keep(mixed)
        there = swapped(total(got[0], mine[0]), "hid", 2)
        pieces.append((got[1].astype(F32) + mine[1].astype(F32) + there.astype(F32)).astype(BF16))
    return jnp.concatenate(pieces[::-1])


def solution(mesh):
    placed = (P("seq", None, "hid"), P(None, None, "hid"), P("hid", None), P("hid"), P("hid", None))
    return jax.shard_map(
        shards, mesh=mesh, in_specs=placed, out_specs=P("seq", "hid"), check_vma=False
    )
```

time: 97.9 us -> 68.5 us (0.70)
  the two profiles are of different devices: /device:TPU:0 before, /device:TPU:2 now
where the time goes in v1:
time: 68.5 us; the launch traced here: 68.2 us
  Pallas kernels  29 us (42%)
  waiting for transfers between devices  23.4 us (34%)
  starting transfers between devices  12 us (18%)
  other arithmetic  2.99 us (4%)
  local copies, waits for them, and re-layouts  0.75 us (1%)
    ppermute x6, waiting for transfers between devices, swapped(): lax.ppermute(array, axis, [(i, i ^ mask) for i in range(lax.axis_size(axi...  16.4 us
    pallas_call x3, Pallas kernels, keep(): pl.pallas_call(functools.partial(keep_kernel, width), name='keep', out_sh...  13.2 us
    ppermute x6, starting transfers between devices, swapped(): lax.ppermute(array, axis, [(i, i ^ mask) for i in range(lax.axis_size(axi...  10.1 us
    pallas_call x2, Pallas kernels, later(): pl.pallas_call(functools.partial(later_kernel, begin, rows, back, width),...  10 us
    ppermute x1, waiting for transfers between devices, shards(): before = lax.ppermute(halo, 'seq', [(i, i + 1) for i in range(span - 1)])  7.03 us
    pallas_call x1, Pallas kernels, shards(): pl.pallas_call(functools.partial(first_kernel, rows1, width), name='first...  5.74 us
    ppermute x1, starting transfers between devices, shards(): before = lax.ppermute(halo, 'seq', [(i, i + 1) for i in range(span - 1)])  1.91 us
  transfers between devices with their start and end apart: 7, of which 4 were waited for; matrix products, arithmetic and copies ran while one was open for 3% of the time, Pallas kernels for 34%

profile of v1, /device:TPU:2, one launch (start us, length us, event | category | flops | bytes accessed | tf_op | source)
XLA Modules:
  0.0 68.2 jit_solution(15784814015168169650)
XLA Ops:
  0.0 5.7 %first.1 = (bf16[2,112,1024]{2,1,0:T(8,128)(2,1)}, bf16[112,1024]{1,0:T(8,128)(2,1)}, bf16[256,1024]{1,0:T(8,128)(2,1)}, bf16[176,1024]{1,0:T(8,128)(2,1)}, f32[256,1024]{1,0:T(8,128)}) custom-call(bf16[3,256,1024]{2,1,0:T(8,128)(2,1)} %bitcast.20, f32[3,3,1024]{2,1,0:T(4,128)} %short.5, bf16[1024,128]{1,0:T(8,128)(2,1)} %long_taps.1, f32[1,1024]{1,0:T(1,128)} %bitcast.23, ...), custom_call_target="tpu_custom_call" | custom-call | tf_op jit(solution)/shard_map/first/pallas_call | solution.py:196
  5.8 1.6 %collective-permute-start.5 = (bf16[2,112,1024]{2,1,0:T(8,128)(2,1)}, bf16[2,112,1024]{2,1,0:T(8,128)(2,1)S(1)}, u32[]{:S(2)}, u32[]{:S(2)}) collective-permute-start(bf16[2,112,1024]{2,1,0:T(8,128)(2,1)} %get-tuple-element.21), channel_id=1, source_target_pairs={{0,1},{1,0},{2,3},{3,2},{4,5},{5,4},{6,7},{7,6},{8,9},{9,8},{10,11... | collective-permute-start | bytes 1376264 | tf_op jit(solution)/shard_map/ppermute | solution.py:177
  7.4 1.9 %collective-permute-start = (bf16[176,1024]{1,0:T(8,128)(2,1)}, bf16[176,1024]{1,0:T(8,128)(2,1)S(1)}, u32[]{:S(2)}, u32[]{:S(2)}) collective-permute-start(bf16[176,1024]{1,0:T(8,128)(2,1)} %get-tuple-element.15), channel_id=1, source_target_pairs={{0,4},{4,8},{8,12},{12,16},{16,20},{20,24},{24,28},{1,5},{5,9},{9,... | collective-permute-start | bytes 1081352 | tf_op jit(solution)/shard_map/ppermute | solution.py:215
  9.3 7.0 %collective-permute-done.halo = bf16[176,1024]{1,0:T(8,128)(2,1)S(1)} collective-permute-done((bf16[176,1024]{1,0:T(8,128)(2,1)}, bf16[176,1024]{1,0:T(8,128)(2,1)S(1)}, u32[]{:S(2)}, u32[]{:S(2)}) %collective-permute-start) | collective-permute-done | bytes 360480 | tf_op jit(solution)/shard_map/ppermute | solution.py:215
  16.3 0.7 %copy-done.1 = bf16[176,1024]{1,0:T(8,128)(2,1)} copy-done((bf16[176,1024]{1,0:T(8,128)(2,1)}, bf16[176,1024]{1,0:T(8,128)(2,1)S(1)}, u32[]{:S(2)}) %copy-start.1) | copy-done | bytes 360472
  17.1 5.0 %later0.1 = (bf16[2,64,1024]{2,1,0:T(8,128)(2,1)}, bf16[64,1024]{1,0:T(8,128)(2,1)}) custom-call(bf16[3,256,1024]{2,1,0:T(8,128)(2,1)} %bitcast.21, f32[3,3,1024]{2,1,0:T(4,128)} %short.5, bf16[256,1024]{1,0:T(8,128)(2,1)} %get-tuple-element.14.gated, bf16[176,1024]{1,0:T(8,128)(2,1)} %copy-done.1, f32[256,1024]{1,0:T(8,128)} %get-tuple-element.16.h, ...), custom_call_target="tpu_custom_call" | custom-call | tf_op jit(solution)/shard_map/later0/pallas_call | solution.py:219
  22.1 0.5 collective-permute-start.1
  22.6 4.4 %keep.5 = bf16[2,112,1024]{2,1,0:T(8,128)(2,1)} custom-call(bf16[112,1024]{1,0:T(8,128)(2,1)} %get-tuple-element.22.mixed, bf16[1024,4096]{1,0:T(8,128)(2,1)} %weight.11), custom_call_target="tpu_custom_call" | custom-call | tf_op jit(solution)/shard_map/keep/pallas_call | solution.py:234
  27.0 5.0 %later64.1 = (bf16[2,80,1024]{2,1,0:T(8,128)(2,1)}, bf16[80,1024]{1,0:T(8,128)(2,1)}) custom-call(bf16[3,256,1024]{2,1,0:T(8,128)(2,1)} %bitcast.22, f32[3,3,1024]{2,1,0:T(4,128)} %short.5, bf16[256,1024]{1,0:T(8,128)(2,1)} %get-tuple-element.14.gated, bf16[176,1024]{1,0:T(8,128)(2,1)} %copy-done.1, f32[256,1024]{1,0:T(8,128)} %get-tuple-element.16.h, ...), custom_call_target="tpu_custom_call" | custom-call | tf_op jit(solution)/shard_map/later64/pallas_call | solution.py:219
  32.1 4.4 %keep.4 = bf16[2,80,1024]{2,1,0:T(8,128)(2,1)} custom-call(bf16[80,1024]{1,0:T(8,128)(2,1)} %get-tuple-element.20.mixed, bf16[1024,4096]{1,0:T(8,128)(2,1)} %weight.11), custom_call_target="tpu_custom_call" | custom-call | tf_op jit(solution)/shard_map/keep/pallas_call | solution.py:234
  36.6 1.6 %collective-permute-start.3 = (bf16[2,80,1024]{2,1,0:T(8,128)(2,1)S(1)}, bf16[2,80,1024]{2,1,0:T(8,128)(2,1)S(1)}, u32[]{:S(2)}, u32[]{:S(2)}) collective-permute-start(bf16[2,80,1024]{2,1,0:T(8,128)(2,1)S(1)} %copy-done.3), channel_id=1, source_target_pairs={{0,1},{1,0},{2,3},{3,2},{4,5},{5,4},{6,7},{7,6},{8,9},{9,8},{10,11... | collective-permute-start | bytes 983048 | tf_op jit(solution)/shard_map/ppermute | solution.py:177
  38.2 4.3 %keep.3 = bf16[2,64,1024]{2,1,0:T(8,128)(2,1)} custom-call(bf16[64,1024]{1,0:T(8,128)(2,1)} %get-tuple-element.18.mixed, bf16[1024,4096]{1,0:T(8,128)(2,1)} %weight.11), custom_call_target="tpu_custom_call" | custom-call | tf_op jit(solution)/shard_map/keep/pallas_call | solution.py:234
  42.6 0.1 fusion.3
  42.6 2.7 %collective-permute-start.6 = (bf16[112,1024]{1,0:T(8,128)(2,1)S(1)}, bf16[112,1024]{1,0:T(8,128)(2,1)S(1)}, u32[]{:S(2)}, u32[]{:S(2)}) collective-permute-start(bf16[112,1024]{1,0:T(8,128)(2,1)S(1)} %fusion.3), channel_id=1, source_target_pairs={{0,2},{1,3},{2,0},{3,1},{4,6},{5,7},{6,4},{7,5},{8,10},{9,11},{10,... | collective-permute-start | bytes 688136 | tf_op jit(solution)/shard_map/ppermute | solution.py:177
  45.3 0.9 %fusion.5 = bf16[64,1024]{1,0:T(8,128)(2,1)S(1)} fusion(bf16[2,64,1024]{2,1,0:T(8,128)(2,1)} %keep.3, bf16[2,64,1024]{2,1,0:T(8,128)(2,1)S(1)} %collective-permute-done.1), kind=kLoop, calls=%fused_computation.12 | loop fusion | flops 262144 | bytes 393216 | tf_op jit(solution)/shard_map/convert_element_type | solution.py:249
  46.2 0.4 collective-permute-start.2
  46.7 3.2 %collective-permute-start.4 = (bf16[80,1024]{1,0:T(8,128)(2,1)S(1)}, bf16[80,1024]{1,0:T(8,128)(2,1)S(1)}, u32[]{:S(2)}, u32[]{:S(2)}) collective-permute-start(bf16[80,1024]{1,0:T(8,128)(2,1)S(1)} %fusion.4), channel_id=1, source_target_pairs={{0,2},{1,3},{2,0},{3,1},{4,6},{5,7},{6,4},{7,5},{8,10},{9,11},{10,... | collective-permute-start | bytes 491528 | tf_op jit(solution)/shard_map/ppermute | solution.py:177
  49.9 12.4 %collective-permute-done.6 = bf16[112,1024]{1,0:T(8,128)(2,1)S(1)} collective-permute-done((bf16[112,1024]{1,0:T(8,128)(2,1)S(1)}, bf16[112,1024]{1,0:T(8,128)(2,1)S(1)}, u32[]{:S(2)}, u32[]{:S(2)}) %collective-permute-start.6) | collective-permute-done | bytes 229408 | tf_op jit(solution)/shard_map/ppermute | solution.py:177
  62.3 0.1 fusion
  62.4 2.7 %collective-permute-done.2 = bf16[64,1024]{1,0:T(8,128)(2,1)S(1)} collective-permute-done((bf16[64,1024]{1,0:T(8,128)(2,1)S(1)}, bf16[64,1024]{1,0:T(8,128)(2,1)S(1)}, u32[]{:S(2)}, u32[]{:S(2)}) %collective-permute-start.2) | collective-permute-done | bytes 131104 | tf_op jit(solution)/shard_map/ppermute | solution.py:177
  65.1 1.0 %fusion.2 = bf16[64,1024]{1,0:T(8,128)(2,1)S(1)} fusion(bf16[64,1024]{1,0:T(8,128)(2,1)S(1)} %collective-permute-done.2, bf16[2,64,1024]{2,1,0:T(8,128)(2,1)} %keep.3, bf16[2,64,1024]{2,1,0:T(8,128)(2,1)S(1)} %collective-permute-done.1), kind=kLoop, calls=%fused_computation.8 | loop fusion | flops 393216 | bytes 524288 | tf_op jit(solution)/shard_map/convert_element_type | solution.py:255
  66.1 1.2 %collective-permute-done.4 = bf16[80,1024]{1,0:T(8,128)(2,1)S(1)} collective-permute-done((bf16[80,1024]{1,0:T(8,128)(2,1)S(1)}, bf16[80,1024]{1,0:T(8,128)(2,1)S(1)}, u32[]{:S(2)}, u32[]{:S(2)}) %collective-permute-start.4) | collective-permute-done | bytes 163872 | tf_op jit(solution)/shard_map/ppermute | solution.py:177
  67.3 0.1 fusion.1
  67.4 0.8 %pad_maximum_fusion = bf16[256,1024]{1,0:T(8,128)(2,1)} fusion(bf16[112,1024]{1,0:T(8,128)(2,1)S(1)} %fusion, bf16[80,1024]{1,0:T(8,128)(2,1)S(1)} %fusion.1, bf16[64,1024]{1,0:T(8,128)(2,1)S(1)} %fusion.2), kind=kLoop, calls=%fused_computation | loop fusion | flops 1572864 | bytes 1048576 | tf_op jit(solution)/shard_map/concatenate | solution.py:256
  (11 shorter events, 0.1 us)
Async XLA Ops:
  5.8 36.8 %collective-permute-start.5 = (bf16[2,112,1024]{2,1,0:T(8,128)(2,1)}, bf16[2,112,1024]{2,1,0:T(8,128)(2,1)S(1)}, u32[]{:S(2)}, u32[]{:S(2)}) collective-permute-start(bf16[2,112,1024]{2,1,0:T(8,128)(2,1)} %get-tuple-element.21), channel_id=1, source_target_pairs={{0,1},{1,0},{2,3},{3,2},{4,5},{5,4},{6,7},{7,6},{8,9},{9,8},{10,11... | collective-permute-start | bytes 1376264 | tf_op jit(solution)/shard_map/ppermute | solution.py:177
  7.4 8.9 %collective-permute-start = (bf16[176,1024]{1,0:T(8,128)(2,1)}, bf16[176,1024]{1,0:T(8,128)(2,1)S(1)}, u32[]{:S(2)}, u32[]{:S(2)}) collective-permute-start(bf16[176,1024]{1,0:T(8,128)(2,1)} %get-tuple-element.15), channel_id=1, source_target_pairs={{0,4},{4,8},{8,12},{12,16},{16,20},{20,24},{24,28},{1,5},{5,9},{9,... | collective-permute-start | bytes 1081352 | tf_op jit(solution)/shard_map/ppermute | solution.py:215
  16.3 0.7 %copy-start.1 = (bf16[176,1024]{1,0:T(8,128)(2,1)}, bf16[176,1024]{1,0:T(8,128)(2,1)S(1)}, u32[]{:S(2)}) copy-start(bf16[176,1024]{1,0:T(8,128)(2,1)S(1)} %collective-permute-done.halo) | copy-start | bytes 1081348
  22.1 23.2 %collective-permute-start.1 = (bf16[2,64,1024]{2,1,0:T(8,128)(2,1)}, bf16[2,64,1024]{2,1,0:T(8,128)(2,1)S(1)}, u32[]{:S(2)}, u32[]{:S(2)}) collective-permute-start(bf16[2,64,1024]{2,1,0:T(8,128)(2,1)} %get-tuple-element.17), channel_id=1, source_target_pairs={{0,1},{1,0},{2,3},{3,2},{4,5},{5,4},{6,7},{7,6},{8,9},{9,8},{10,11... | collective-permute-start | bytes 786440 | tf_op jit(solution)/shard_map/ppermute | solution.py:177
  32.1 4.5 %copy-start.3 = (bf16[2,80,1024]{2,1,0:T(8,128)(2,1)S(1)}, bf16[2,80,1024]{2,1,0:T(8,128)(2,1)}, u32[]{:S(2)}) copy-start(bf16[2,80,1024]{2,1,0:T(8,128)(2,1)} %get-tuple-element.19) | copy-start | bytes 983044
  32.1 10.5 %copy-start = (bf16[2,112,1024]{2,1,0:T(8,128)(2,1)S(1)}, bf16[2,112,1024]{2,1,0:T(8,128)(2,1)}, u32[]{:S(2)}) copy-start(bf16[2,112,1024]{2,1,0:T(8,128)(2,1)} %keep.5) | copy-start | bytes 1376260
  36.5 10.1 %copy-start.2 = (bf16[2,80,1024]{2,1,0:T(8,128)(2,1)S(1)}, bf16[2,80,1024]{2,1,0:T(8,128)(2,1)}, u32[]{:S(2)}) copy-start(bf16[2,80,1024]{2,1,0:T(8,128)(2,1)} %keep.4) | copy-start | bytes 983044
  36.6 10.1 %collective-permute-start.3 = (bf16[2,80,1024]{2,1,0:T(8,128)(2,1)S(1)}, bf16[2,80,1024]{2,1,0:T(8,128)(2,1)S(1)}, u32[]{:S(2)}, u32[]{:S(2)}) collective-permute-start(bf16[2,80,1024]{2,1,0:T(8,128)(2,1)S(1)} %copy-done.3), channel_id=1, source_target_pairs={{0,1},{1,0},{2,3},{3,2},{4,5},{5,4},{6,7},{7,6},{8,9},{9,8},{10,11... | collective-permute-start | bytes 983048 | tf_op jit(solution)/shard_map/ppermute | solution.py:177
  42.6 19.7 %collective-permute-start.6 = (bf16[112,1024]{1,0:T(8,128)(2,1)S(1)}, bf16[112,1024]{1,0:T(8,128)(2,1)S(1)}, u32[]{:S(2)}, u32[]{:S(2)}) collective-permute-start(bf16[112,1024]{1,0:T(8,128)(2,1)S(1)} %fusion.3), channel_id=1, source_target_pairs={{0,2},{1,3},{2,0},{3,1},{4,6},{5,7},{6,4},{7,5},{8,10},{9,11},{10,... | collective-permute-start | bytes 688136 | tf_op jit(solution)/shard_map/ppermute | solution.py:177
  46.2 18.9 %collective-permute-start.2 = (bf16[64,1024]{1,0:T(8,128)(2,1)S(1)}, bf16[64,1024]{1,0:T(8,128)(2,1)S(1)}, u32[]{:S(2)}, u32[]{:S(2)}) collective-permute-start(bf16[64,1024]{1,0:T(8,128)(2,1)S(1)} %fusion.5), channel_id=1, source_target_pairs={{0,2},{1,3},{2,0},{3,1},{4,6},{5,7},{6,4},{7,5},{8,10},{9,11},{10,... | collective-permute-start | bytes 393224 | tf_op jit(solution)/shard_map/ppermute | solution.py:177
  46.7 20.6 %collective-permute-start.4 = (bf16[80,1024]{1,0:T(8,128)(2,1)S(1)}, bf16[80,1024]{1,0:T(8,128)(2,1)S(1)}, u32[]{:S(2)}, u32[]{:S(2)}) collective-permute-start(bf16[80,1024]{1,0:T(8,128)(2,1)S(1)} %fusion.4), channel_id=1, source_target_pairs={{0,2},{1,3},{2,0},{3,1},{4,6},{5,7},{6,4},{7,5},{8,10},{9,11},{10,... | collective-permute-start | bytes 491528 | tf_op jit(solution)/shard_map/ppermute | solution.py:177

commit v2 on v0

v2 whole, which is shorter than its diff:
```python
import functools

import jax
import jax.numpy as jnp
import numpy as np
from jax import lax
from jax.experimental import pallas as pl
from jax.experimental.pallas import tpu as pltpu
from jax.sharding import PartitionSpec as P


F32 = jnp.float32
BF16 = jnp.bfloat16
PAD = 16
STRIP = 256
LAST = 64
VMEM_LIMIT = 40 << 20
LAST = 64
VMEM_LIMIT = 40 << 20
ANY = pl.BlockSpec(memory_space=pl.ANY)
VMEM = pl.BlockSpec(memory_space=pltpu.VMEM)
VMEM = pl.BlockSpec(memory_space=pltpu.VMEM)


def split(values):
    high = values.astype(BF16)
    return high, (values - high.astype(F32)).astype(BF16)


def transforms(length):
    size = 2 * length
    angle = np.pi * (2 * np.arange(length)[:, None] + 1) * np.arange(size)[None] / size
    forward = np.concatenate([np.cos(angle), -np.sin(angle)])
    inverse = forward.T[length:] / length

    def halves(matrix):
        high = matrix.astype(BF16)
        return jnp.asarray(np.concatenate([high, (matrix - high.astype(np.float64)).astype(BF16)]))

    return halves(forward), halves(inverse)


def matmul(a, b):
    return jnp.dot(a, b, preferred_element_type=F32)


def short_filter(ext, taps, rows):
    total = ext.shape[0]
    one = pltpu.roll(ext, 1, 0)
    two = pltpu.roll(ext, 2, 0)
    out = taps[0:1] * ext + taps[1:2] * one + taps[2:3] * two
    return out[total - rows :]


def spectrum_product(x, h):
    half = x.shape[0] // 2
    xr, xi, hr, hi = x[:half], x[half:], h[:half], h[half:]
    return jnp.concatenate([xr * hr - xi * hi, xr * hi + xi * hr])


def both(stacked):
    half = stacked.shape[0] // 2
    return stacked[:half] + stacked[half:]


def filter_window(window, h, fwd, inv, first, rows):
    length = inv.shape[0] // 2
    high, low = split(spectrum_product(both(matmul(fwd[...], window)), h))
    inv_hi = inv[first : first + rows]
    inv_lo = inv[length + first : length + first + rows]
    return both(matmul(jnp.concatenate([inv_hi, inv_lo]), high)) + matmul(inv_hi, low)


def columns(ref, which, width):
    return ref[:, pl.ds(pl.multiple_of(which * width, width), width)]


def first_kernel(
    rows, width, proj_hbm, short_hbm, long_hbm, skip_hbm, fwd_hbm, inv_hbm, w_hbm,
    pay, mixed, gated, halo, h, q, head, short, fwd, inv, w,
    k_buf, v_buf, long_buf, skip_buf, sems,
):
    me = lax.axis_index("hid")
    tokens, channels = k_buf.shape
    length = long_buf.shape[1]
    pairs = [
        (short_hbm, short), (proj_hbm.at[1], k_buf), (proj_hbm.at[2], v_buf), (fwd_hbm, fwd), (long_hbm, long_buf),
        (skip_hbm, skip_buf), (proj_hbm.at[0], q), (inv_hbm, inv), (w_hbm, w),
    ]
    copies = [pltpu.make_async_copy(src, dst, sems.at[i]) for i, (src, dst) in enumerate(pairs)]
    for copy in copies:
        copy.start()
    for copy in copies[:-1]:
        copy.wait()
    row = lax.broadcasted_iota(jnp.int32, (tokens, STRIP), 0)
    for at in range(0, channels, STRIP):
        part = slice(at, at + STRIP)
        key = short_filter(k_buf[:, part].astype(F32), short[:, 1, part], tokens)
        value = short_filter(v_buf[:, part].astype(F32), short[:, 2, part], tokens)
        window = jnp.where(row < 2, 0.0, key * value).astype(BF16)
        gated[:, part] = window
        contract = (((1,), (1,)), ((), ()))
        taps = both(lax.dot_general(fwd[:, :length], long_buf[part], contract, preferred_element_type=F32))
        spectrum = jnp.concatenate([taps[:length] + skip_buf[:, part], taps[length:]])
        h[:, part] = spectrum
        filtered = filter_window(window, spectrum, fwd, inv, length - rows, rows)
        query = short_filter(q[tokens - rows - PAD :, part].astype(F32), short[:, 0, part], rows)
        mixed[:, part] = (query * filtered).astype(BF16)
    halo[:length] = gated[tokens - length :]
    halo[length : length + PAD] = q[tokens - PAD :]
    halo[length + PAD : length + 2 * PAD] = k_buf[tokens - PAD :]
    halo[length + 2 * PAD :] = v_buf[tokens - PAD :]
    head[0] = k_buf[:PAD]
    head[1] = v_buf[:PAD]
    copies[-1].wait()
    pay[0] = matmul(mixed[...], columns(w, me ^ 3, width)).astype(BF16)
    pay[1] = matmul(mixed[...], columns(w, me ^ 1, width)).astype(BF16)


def later_kernel(begin, rows, back, width, halo, gated, h, q, head, short, fwd, inv, w, pay, mixed):
    me = lax.axis_index("hid")
    length, channels = halo.shape[0] - 3 * PAD, halo.shape[1]
    for at in range(0, channels, STRIP):
        part = slice(at, at + STRIP)

        def led(which, own):
            before = halo[length + which * PAD : length + (which + 1) * PAD, part].astype(F32)
            return jnp.concatenate([before, own.astype(F32)])

        key = short_filter(led(1, head[0, :, part]), short[:, 1, part], PAD)
        value = short_filter(led(2, head[1, :, part]), short[:, 2, part], PAD)
        fixed = (key * value).astype(BF16)
        window = jnp.concatenate([halo[length - back : length, part], fixed, gated[PAD : 2 * length - back, part]])
        filtered = filter_window(window, h[:, part], fwd, inv, begin + back - length, rows)
        if begin:
            ext = q[begin - PAD : begin + rows, part].astype(F32)
        else:
            ext = led(0, q[:rows, part])
        query = short_filter(ext, short[:, 0, part], rows)
        mixed[:, part] = (query * filtered).astype(BF16)
    pay[0] = matmul(mixed[...], columns(w, me ^ 3, width)).astype(BF16)
    pay[1] = matmul(mixed[...], columns(w, me ^ 1, width)).astype(BF16)


def keep_kernel(width, count, *refs):
    me = lax.axis_index("hid")
    mixed, w, outs = refs[:count], refs[count], refs[count + 1 :]
    rows = jnp.concatenate([m[...] for m in mixed]) if count > 1 else mixed[0][...]
    for slot, which in ((0, me ^ 2), (1, me)):
        result = matmul(rows, columns(w, which, width)).astype(BF16)
        at = 0
        for out in outs:
            out[slot] = result[at : at + out.shape[1]]
            at += out.shape[1]


def call(kernel, outs, args, in_specs=None, scratch=()):
    if in_specs is None:
        in_specs = [VMEM] * len(args)
        args = [pltpu.with_memory_space_constraint(a, pltpu.VMEM) for a in args]
    return pl.pallas_call(
        kernel,
        out_shape=tuple(pltpu.VMEM(dims, dtype) for dims, dtype in outs),
        in_specs=in_specs,
        out_specs=(VMEM,) * len(outs),
        scratch_shapes=scratch,
        compiler_params=pltpu.CompilerParams(vmem_limit_bytes=VMEM_LIMIT),
    )(*args)


def swapped(array, mask):
    return lax.ppermute(array, "hid", [(i, i ^ mask) for i in range(lax.axis_size("hid"))])


def total(a, b):
    return (a.astype(F32) + b.astype(F32)).astype(BF16)


def mixer(projected, short_taps, long_taps, skip_gain, out_weight):
    tokens, _, channels = projected.shape
    length = long_taps.shape[1]
    width = out_weight.shape[1] // lax.axis_size("hid")
    proj = jnp.transpose(projected, (1, 0, 2))
    fwd, inv = transforms(length)
    size = 2 * length
    rows1 = tokens - length - PAD
    rows3 = LAST
    rows2 = tokens - rows1 - rows3

    pay1, mixed1, gated, halo, h, q, head, short, fwd, inv, w = call(
        functools.partial(first_kernel, rows1, width),
        [
            ((2, rows1, width), BF16), ((rows1, channels), BF16), ((tokens, channels), BF16),
            ((length + 3 * PAD, channels), BF16), ((size, channels), F32), ((tokens, channels), BF16),
            ((2, PAD, channels), BF16), (short_taps.shape, F32), (fwd.shape, BF16), (inv.shape, BF16),
            (out_weight.shape, BF16),
        ],
        [
            pltpu.with_memory_space_constraint(a, pltpu.HBM)
            for a in (proj, short_taps, long_taps, skip_gain[None], fwd, inv, out_weight)
        ],
        [ANY] * 7,
        [
            pltpu.VMEM((tokens, channels), BF16), pltpu.VMEM((tokens, channels), BF16),
            pltpu.VMEM(long_taps.shape, BF16), pltpu.VMEM((1, channels), F32), pltpu.SemaphoreType.DMA((9,)),
        ],
    )
    got1 = swapped(pay1, 1)
    before = lax.ppermute(halo, "seq", [(i, i + 1) for i in range(lax.axis_size("seq") - 1)])

    def later(begin, rows, back):
        return call(
            functools.partial(later_kernel, begin, rows, back, width),
            [((2, rows, width), BF16), ((rows, channels), BF16)],
            (before, gated, h, q, head, short, fwd, inv, w),
        )

    def keep(*mixed):
        return call(
            functools.partial(keep_kernel, width, len(mixed)),
            [((2, m.shape[0], width), BF16) for m in mixed],
            (*mixed, w),
        )

    (keep1,) = keep(mixed1)
    pay2, mixed2 = later(rows3, rows2, length - PAD)
    got2 = swapped(pay2, 1)
    pay3, mixed3 = later(0, rows3, length)
    got3 = swapped(pay3, 1)
    keep2, keep3 = keep(mixed2, mixed3)

    pieces = []
    for got, mine in ((got1, keep1), (got2, keep2), (got3, keep3)):
        there = swapped(total(got[0], mine[0]), 2)
        pieces.append((got[1].astype(F32) + mine[1].astype(F32) + there.astype(F32)).astype(BF16))
    return jnp.concatenate(pieces[::-1])


def solution(mesh):
    placed = (P("seq", None, "hid"), P(None, None, "hid"), P("hid", None), P("hid"), P("hid", None))
    return jax.shard_map(mixer, mesh=mesh, in_specs=placed, out_specs=P("seq", "hid"), check_vma=False)
```

time: 97.9 us -> 51.1 us (0.52)
  the two profiles are of different devices: /device:TPU:0 before, /device:TPU:2 now
where the time goes in v2:
time: 51.1 us; the launch traced here: 50.9 us
  waiting for transfers between devices  30.1 us (59%)
  Pallas kernels  10.6 us (21%)
  starting transfers between devices  8.92 us (17%)
  other arithmetic  1.17 us (2%)
    ppermute x6, waiting for transfers between devices, swapped(): lax.ppermute(array, 'hid', [(i, i ^ mask) for i in range(lax.axis_size('h...  23.3 us
    pallas_call x5, Pallas kernels, call(): pl.pallas_call(kernel, out_shape=tuple((pltpu.VMEM(dims, dtype) for dims,...  10.6 us
    ppermute x6, starting transfers between devices, swapped(): lax.ppermute(array, 'hid', [(i, i ^ mask) for i in range(lax.axis_size('h...  7.01 us
    ppermute x1, waiting for transfers between devices, mixer(): lax.ppermute(halo, 'seq', [(i, i + 1) for i in range(lax.axis_size('seq')...  6.82 us
    ppermute x1, starting transfers between devices, mixer(): lax.ppermute(halo, 'seq', [(i, i + 1) for i in range(lax.axis_size('seq')...  1.91 us
  transfers between devices with their start and end apart: 7, of which 5 were waited for; matrix products, arithmetic and copies ran while one was open for 1% of the time, Pallas kernels for 11%

profile of v2, /device:TPU:2, one launch (start us, length us, event | category | flops | bytes accessed | tf_op | source)
XLA Modules:
  0.0 50.9 jit_solution(11351172991564371122)
XLA Ops:
  0.0 5.0 %shard_map.73 = (bf16[2,112,1024]{2,1,0:T(8,128)(2,1)S(1)}, bf16[112,1024]{1,0:T(8,128)(2,1)S(1)}, bf16[256,1024]{1,0:T(8,128)(2,1)S(1)}, bf16[176,1024]{1,0:T(8...) custom-call(bf16[3,256,1024]{2,1,0:T(8,128)(2,1)} %bitcast.20, ...), custom_call_target="tpu_custom_call" | custom-call | tf_op jit(solution)/shard_map/pallas_call | solution.py:161
  5.0 1.6 %collective-permute-start.5 = (bf16[2,112,1024]{2,1,0:T(8,128)(2,1)S(1)}, bf16[2,112,1024]{2,1,0:T(8,128)(2,1)S(1)}, u32[]{:S(2)}, u32[]{:S(2)}) collective-permute-start(bf16[2,112,1024]{2,1,0:T(8,128)(2,1)S(1)} %get-tuple-element.37), channel_id=1, source_target_pairs={{0,1},{1,0},{2,3},{3,2},{4,5},{5,4},{6,7},{7,6},{8,9},{9,8},{10,11... | collective-permute-start | bytes 1376264 | tf_op jit(solution)/shard_map/ppermute | solution.py:172
  6.6 1.9 %collective-permute-start = (bf16[176,1024]{1,0:T(8,128)(2,1)S(1)}, bf16[176,1024]{1,0:T(8,128)(2,1)S(1)}, u32[]{:S(2)}, u32[]{:S(2)}) collective-permute-start(bf16[176,1024]{1,0:T(8,128)(2,1)S(1)} %get-tuple-element.22), channel_id=1, source_target_pairs={{0,4},{4,8},{8,12},{12,16},{16,20},{20,24},{24,28},{1,5},{5,9},{9,... | collective-permute-start | bytes 1081352 | tf_op jit(solution)/shard_map/ppermute | solution.py:209
  8.5 6.8 %collective-permute-done.halo = bf16[176,1024]{1,0:T(8,128)(2,1)S(1)} collective-permute-done((bf16[176,1024]{1,0:T(8,128)(2,1)S(1)}, bf16[176,1024]{1,0:T(8,128)(2,1)S(1)}, u32[]{:S(2)}, u32[]{:S(2)}) %collective-permute-start) | collective-permute-done | bytes 360480 | tf_op jit(solution)/shard_map/ppermute | solution.py:209
  15.3 2.1 %shard_map.74 = (bf16[2,64,1024]{2,1,0:T(8,128)(2,1)S(1)}, bf16[64,1024]{1,0:T(8,128)(2,1)S(1)}) custom-call(bf16[176,1024]{1,0:T(8,128)(2,1)S(1)} %collective-permute-done.halo, bf16[256,1024]{1,0:T(8,128)(2,1)S(1)} %get-tuple-element.23.gated, f32[256,1024]{1,0:T(8,128)S(1)} %get-tuple-element.24.h, bf16[256,1024]{1,0:T(8,128)(2,1)S(1)} %get-tuple-element.25.q, ...), custom_call_target="tpu_custom_call" | custom-call | tf_op jit(solution)/shard_map/pallas_call | solution.py:161
  17.4 0.5 %collective-permute-start.1 = (bf16[2,64,1024]{2,1,0:T(8,128)(2,1)S(1)}, bf16[2,64,1024]{2,1,0:T(8,128)(2,1)S(1)}, u32[]{:S(2)}, u32[]{:S(2)}) collective-permute-start(bf16[2,64,1024]{2,1,0:T(8,128)(2,1)S(1)} %get-tuple-element.31), channel_id=1, source_target_pairs={{0,1},{1,0},{2,3},{3,2},{4,5},{5,4},{6,7},{7,6},{8,9},{9,8},{10,11... | collective-permute-start | bytes 786440 | tf_op jit(solution)/shard_map/ppermute | solution.py:172
  17.9 0.8 %shard_map.77 = bf16[2,112,1024]{2,1,0:T(8,128)(2,1)S(1)} custom-call(bf16[112,1024]{1,0:T(8,128)(2,1)S(1)} %get-tuple-element.38.refs_0_, bf16[1024,4096]{1,0:T(8,128)(2,1)S(1)} %get-tuple-element.30.w.refs_2_.refs_1_), custom_call_target="tpu_custom_call" | custom-call | tf_op jit(solution)/shard_map/pallas_call | solution.py:161
  18.7 2.1 %shard_map.75 = (bf16[2,80,1024]{2,1,0:T(8,128)(2,1)S(1)}, bf16[80,1024]{1,0:T(8,128)(2,1)S(1)}) custom-call(bf16[176,1024]{1,0:T(8,128)(2,1)S(1)} %collective-permute-done.halo, bf16[256,1024]{1,0:T(8,128)(2,1)S(1)} %get-tuple-element.23.gated, f32[256,1024]{1,0:T(8,128)S(1)} %get-tuple-element.24.h, bf16[256,1024]{1,0:T(8,128)(2,1)S(1)} %get-tuple-element.25.q, ...), custom_call_target="tpu_custom_call" | custom-call | tf_op jit(solution)/shard_map/pallas_call | solution.py:161
  20.8 1.6 %collective-permute-start.3 = (bf16[2,80,1024]{2,1,0:T(8,128)(2,1)S(1)}, bf16[2,80,1024]{2,1,0:T(8,128)(2,1)S(1)}, u32[]{:S(2)}, u32[]{:S(2)}) collective-permute-start(bf16[2,80,1024]{2,1,0:T(8,128)(2,1)S(1)} %get-tuple-element.35), channel_id=1, source_target_pairs={{0,1},{1,0},{2,3},{3,2},{4,5},{5,4},{6,7},{7,6},{8,9},{9,8},{10,11... | collective-permute-start | bytes 983048 | tf_op jit(solution)/shard_map/ppermute | solution.py:172
  22.4 0.8 %shard_map.76 = (bf16[2,80,1024]{2,1,0:T(8,128)(2,1)S(1)}, bf16[2,64,1024]{2,1,0:T(8,128)(2,1)S(1)}) custom-call(bf16[80,1024]{1,0:T(8,128)(2,1)S(1)} %get-tuple-element.32.refs_0_, bf16[64,1024]{1,0:T(8,128)(2,1)S(1)} %get-tuple-element.33.refs_1_, bf16[1024,4096]{1,0:T(8,128)(2,1)S(1)} %get-tuple-element.30.w.refs_2_.refs_1_), custom_call_target="tpu_custom_call" | custom-call | tf_op jit(solution)/shard_map/pallas_call | solution.py:161
  23.2 0.0 collective-permute-done.5
  23.2 0.1 fusion.3
  23.3 2.7 %collective-permute-start.6 = (bf16[112,1024]{1,0:T(8,128)(2,1)S(1)}, bf16[112,1024]{1,0:T(8,128)(2,1)S(1)}, u32[]{:S(2)}, u32[]{:S(2)}) collective-permute-start(bf16[112,1024]{1,0:T(8,128)(2,1)S(1)} %fusion.3), channel_id=1, source_target_pairs={{0,2},{1,3},{2,0},{3,1},{4,6},{5,7},{6,4},{7,5},{8,10},{9,11},{10,... | collective-permute-start | bytes 688136 | tf_op jit(solution)/shard_map/ppermute | solution.py:172
  25.9 7.0 %collective-permute-done.1 = bf16[2,64,1024]{2,1,0:T(8,128)(2,1)S(1)} collective-permute-done((bf16[2,64,1024]{2,1,0:T(8,128)(2,1)S(1)}, bf16[2,64,1024]{2,1,0:T(8,128)(2,1)S(1)}, u32[]{:S(2)}, u32[]{:S(2)}) %collective-permute-start.1) | collective-permute-done | bytes 262176 | tf_op jit(solution)/shard_map/ppermute | solution.py:172
  33.0 0.1 collective-permute-start.2
  33.1 5.1 %collective-permute-done.3 = bf16[2,80,1024]{2,1,0:T(8,128)(2,1)S(1)} collective-permute-done((bf16[2,80,1024]{2,1,0:T(8,128)(2,1)S(1)}, bf16[2,80,1024]{2,1,0:T(8,128)(2,1)S(1)}, u32[]{:S(2)}, u32[]{:S(2)}) %collective-permute-start.3) | collective-permute-done | bytes 327712 | tf_op jit(solution)/shard_map/ppermute | solution.py:172
  38.3 0.5 collective-permute-start.4
  38.7 0.0 collective-permute-done.6
  38.8 0.1 fusion
  38.9 9.0 %collective-permute-done.2 = bf16[64,1024]{1,0:T(8,128)(2,1)S(1)} collective-permute-done((bf16[64,1024]{1,0:T(8,128)(2,1)S(1)}, bf16[64,1024]{1,0:T(8,128)(2,1)S(1)}, u32[]{:S(2)}, u32[]{:S(2)}) %collective-permute-start.2) | collective-permute-done | bytes 131104 | tf_op jit(solution)/shard_map/ppermute | solution.py:172
  47.8 0.1 fusion.2
  47.9 2.1 %collective-permute-done.4 = bf16[80,1024]{1,0:T(8,128)(2,1)S(1)} collective-permute-done((bf16[80,1024]{1,0:T(8,128)(2,1)S(1)}, bf16[80,1024]{1,0:T(8,128)(2,1)S(1)}, u32[]{:S(2)}, u32[]{:S(2)}) %collective-permute-start.4) | collective-permute-done | bytes 163872 | tf_op jit(solution)/shard_map/ppermute | solution.py:172
  50.0 0.1 fusion.1
  50.1 0.8 %pad_maximum_fusion = bf16[256,1024]{1,0:T(8,128)(2,1)} fusion(bf16[112,1024]{1,0:T(8,128)(2,1)S(1)} %fusion, bf16[80,1024]{1,0:T(8,128)(2,1)S(1)} %fusion.1, bf16[64,1024]{1,0:T(8,128)(2,1)S(1)} %fusion.2), kind=kLoop, calls=%fused_computation | loop fusion | flops 1572864 | bytes 1048576 | tf_op jit(solution)/shard_map/concatenate | solution.py:236
  (2 shorter events, 0.1 us)
Async XLA Ops:
  5.0 18.3 %collective-permute-start.5 = (bf16[2,112,1024]{2,1,0:T(8,128)(2,1)S(1)}, bf16[2,112,1024]{2,1,0:T(8,128)(2,1)S(1)}, u32[]{:S(2)}, u32[]{:S(2)}) collective-permute-start(bf16[2,112,1024]{2,1,0:T(8,128)(2,1)S(1)} %get-tuple-element.37), channel_id=1, source_target_pairs={{0,1},{1,0},{2,3},{3,2},{4,5},{5,4},{6,7},{7,6},{8,9},{9,8},{10,11... | collective-permute-start | bytes 1376264 | tf_op jit(solution)/shard_map/ppermute | solution.py:172
  6.6 8.7 %collective-permute-start = (bf16[176,1024]{1,0:T(8,128)(2,1)S(1)}, bf16[176,1024]{1,0:T(8,128)(2,1)S(1)}, u32[]{:S(2)}, u32[]{:S(2)}) collective-permute-start(bf16[176,1024]{1,0:T(8,128)(2,1)S(1)} %get-tuple-element.22), channel_id=1, source_target_pairs={{0,4},{4,8},{8,12},{12,16},{16,20},{20,24},{24,28},{1,5},{5,9},{9,... | collective-permute-start | bytes 1081352 | tf_op jit(solution)/shard_map/ppermute | solution.py:209
  17.4 15.6 %collective-permute-start.1 = (bf16[2,64,1024]{2,1,0:T(8,128)(2,1)S(1)}, bf16[2,64,1024]{2,1,0:T(8,128)(2,1)S(1)}, u32[]{:S(2)}, u32[]{:S(2)}) collective-permute-start(bf16[2,64,1024]{2,1,0:T(8,128)(2,1)S(1)} %get-tuple-element.31), channel_id=1, source_target_pairs={{0,1},{1,0},{2,3},{3,2},{4,5},{5,4},{6,7},{7,6},{8,9},{9,8},{10,11... | collective-permute-start | bytes 786440 | tf_op jit(solution)/shard_map/ppermute | solution.py:172
  20.8 17.4 %collective-permute-start.3 = (bf16[2,80,1024]{2,1,0:T(8,128)(2,1)S(1)}, bf16[2,80,1024]{2,1,0:T(8,128)(2,1)S(1)}, u32[]{:S(2)}, u32[]{:S(2)}) collective-permute-start(bf16[2,80,1024]{2,1,0:T(8,128)(2,1)S(1)} %get-tuple-element.35), channel_id=1, source_target_pairs={{0,1},{1,0},{2,3},{3,2},{4,5},{5,4},{6,7},{7,6},{8,9},{9,8},{10,11... | collective-permute-start | bytes 983048 | tf_op jit(solution)/shard_map/ppermute | solution.py:172
  23.3 15.5 %collective-permute-start.6 = (bf16[112,1024]{1,0:T(8,128)(2,1)S(1)}, bf16[112,1024]{1,0:T(8,128)(2,1)S(1)}, u32[]{:S(2)}, u32[]{:S(2)}) collective-permute-start(bf16[112,1024]{1,0:T(8,128)(2,1)S(1)} %fusion.3), channel_id=1, source_target_pairs={{0,2},{1,3},{2,0},{3,1},{4,6},{5,7},{6,4},{7,5},{8,10},{9,11},{10,... | collective-permute-start | bytes 688136 | tf_op jit(solution)/shard_map/ppermute | solution.py:172
  33.0 14.8 %collective-permute-start.2 = (bf16[64,1024]{1,0:T(8,128)(2,1)S(1)}, bf16[64,1024]{1,0:T(8,128)(2,1)S(1)}, u32[]{:S(2)}, u32[]{:S(2)}) collective-permute-start(bf16[64,1024]{1,0:T(8,128)(2,1)S(1)} %fusion.5), channel_id=1, source_target_pairs={{0,2},{1,3},{2,0},{3,1},{4,6},{5,7},{6,4},{7,5},{8,10},{9,11},{10,... | collective-permute-start | bytes 393224 | tf_op jit(solution)/shard_map/ppermute | solution.py:172
  38.3 11.7 %collective-permute-start.4 = (bf16[80,1024]{1,0:T(8,128)(2,1)S(1)}, bf16[80,1024]{1,0:T(8,128)(2,1)S(1)}, u32[]{:S(2)}, u32[]{:S(2)}) collective-permute-start(bf16[80,1024]{1,0:T(8,128)(2,1)S(1)} %fusion.4), channel_id=1, source_target_pairs={{0,2},{1,3},{2,0},{3,1},{4,6},{5,7},{6,4},{7,5},{8,10},{9,11},{10,... | collective-permute-start | bytes 491528 | tf_op jit(solution)/shard_map/ppermute | solution.py:172
